TPU v7x, 32 devices: a whole 2x2x4 slice. The times are simulated.
32 devices in a mesh: seq: 8 (over z, y), head: 2 (over x), dp: 2 (over core).
Axes of the slice: x: 2, y: 2, z: 4, core: 2. Of those that a mesh axis runs over, the one named last changes fastest.
Arguments:
- queries: bfloat16 [2048, 4096], P(('dp', 'seq'), 'head'), parts along dimension 0, may hold values from -6 to 6
- key_vectors: bfloat16 [2048, 4096], P(('dp', 'seq'), 'head'), parts along dimension 0, may hold values from -6 to 6
- value_vectors: bfloat16 [2048, 4096], P(('dp', 'seq'), 'head'), parts along dimension 0, may hold values from -6 to 6
- grad_out: bfloat16 [2048, 4096], P(('dp', 'seq'), 'head'), parts along dimension 0, may hold values from -6 to 6
Outputs:
- grad_queries: bfloat16 [2048, 4096], P(('dp', 'seq'), 'head'), parts along dimension 0
- grad_keys: bfloat16 [2048, 4096], P(('dp', 'seq'), 'head'), parts along dimension 0
- grad_values: bfloat16 [2048, 4096], P(('dp', 'seq'), 'head'), parts along dimension 0
There are 2 independent parts, one for each index of `dp`. A program takes and returns all parts, laid end to end along the dimension named above; each array names one. Nothing has to cross between parts.
All inputs are finite; a program needn't handle non-finite values.
Results may differ from a plain program's by a relative error of at most 0.012.
Values may be sent and summed in bfloat16 or wider, within the bound.
No kernel may reach another device: no remote copies, remote signals or barrier semaphores. Data moves between devices by JAX's collectives and lax.ppermute only.
A program may use at most 128 MiB of HBM per device.

v0:
```python
import jax
import jax.numpy as jnp
from jax import lax
from jax.sharding import PartitionSpec as P

E = 128
B = 128
masked_value = -1e30


def passed_along(block, axis, distance):
    devices = range(lax.axis_size(axis))
    route = [(i - distance, i) for i in devices if i - distance in devices]
    return lax.ppermute(block, axis, route)


def prefix(part, axis, combine, identity):
    count = lax.axis_size(axis)
    place = lax.axis_index(axis)
    ahead = count - 1 - place
    gathered = jax.tree.map(lambda a: lax.all_gather(a, axis), part)
    state = jax.tree.map(lambda a, e: jnp.zeros_like(a) + jnp.asarray(e, a.dtype), part, identity)

    def one(turn, state):
        source = count - 1 - turn
        return combine(
            state, jax.tree.map(lambda a: lax.dynamic_index_in_dim(a, source, 0, False), gathered)
        )

    return lax.fori_loop(0, ahead, one, state)


def scores(query_part, key_part, allowed):
    scaling = query_part.shape[2] ** (-0.5)
    logits = (
        jnp.einsum("qhe,khe->hqk", query_part, key_part, preferred_element_type=jnp.float32)
        * scaling
    )
    return jnp.where(allowed[None], logits, masked_value)


def backward_terms(query_part, value_part, grad_part, logits, log_total, inner_term):
    scaling = query_part.shape[2] ** (-0.5)
    probs = jnp.exp(logits - log_total)
    probs_low = probs.astype(jnp.bfloat16)
    grad_probs = jnp.einsum(
        "qhe,khe->hqk", grad_part, value_part, preferred_element_type=jnp.float32
    )
    grad_logits = (probs * (grad_probs - inner_term)).astype(jnp.bfloat16)
    grad_keyset = scaling * jnp.einsum(
        "hqk,qhe->khe", grad_logits, query_part, preferred_element_type=jnp.float32
    )
    grad_valset = jnp.einsum(
        "hqk,qhe->khe", probs_low, grad_part, preferred_element_type=jnp.float32
    )
    return (grad_logits, grad_keyset, grad_valset)


def attend_back(query_part, key_part, value_part, grad_part, allowed):
    scaling = query_part.shape[2] ** (-0.5)
    logits = scores(query_part, key_part, allowed)
    row_max = jnp.max(logits, axis=2, keepdims=True)
    log_total = row_max + jnp.log(jnp.sum(jnp.exp(logits - row_max), axis=2, keepdims=True))
    probs_low = jnp.exp(logits - log_total).astype(jnp.bfloat16)
    output = jnp.einsum("hqk,khe->qhe", probs_low, value_part, preferred_element_type=jnp.float32)
    inner_term = jnp.einsum("qhe,qhe->hq", grad_part.astype(jnp.float32), output)[:, :, None]
    grad_logits, grad_keyset, grad_valset = backward_terms(
        query_part, value_part, grad_part, logits, log_total, inner_term
    )
    grad_query = scaling * jnp.einsum(
        "hqk,khe->qhe", grad_logits, key_part, preferred_element_type=jnp.float32
    )
    return (grad_query, grad_keyset, grad_valset, log_total, inner_term)


def add_pair(earlier, later):
    return (earlier[0] + later[0], earlier[1] + later[1])


def body(queries, key_vectors, value_vectors, grad_out):
    shard_len, feature_count = queries.shape
    head_count = feature_count // E
    block_count = shard_len // B
    offset = lax.axis_index("seq") * shard_len
    query_heads = queries.reshape(shard_len, head_count, E)
    key_heads = key_vectors.reshape(shard_len, head_count, E)
    value_heads = value_vectors.reshape(shard_len, head_count, E)
    grad_heads = grad_out.reshape(shard_len, head_count, E)
    halo_key, halo_value = passed_along((key_heads, value_heads), "seq", 1)
    key_blocks = key_heads.reshape(block_count, B, head_count, E)
    value_blocks = value_heads.reshape(block_count, B, head_count, E)
    query_blocks = query_heads.reshape(block_count, B, head_count, E)
    grad_blocks = grad_heads.reshape(block_count, B, head_count, E)
    strided_key = key_blocks[:, B - 1]
    strided_value = value_blocks[:, B - 1]
    summary_key, summary_value = (
        lax.all_gather(strided_key, "seq", axis=0, tiled=True),
        lax.all_gather(strided_value, "seq", axis=0, tiled=True),
    )
    summary_count = summary_key.shape[0]
    key_before = jnp.concatenate([halo_key[None], key_blocks[:-1]], axis=0)
    value_before = jnp.concatenate([halo_value[None], value_blocks[:-1]], axis=0)
    steps_b = jnp.arange(B, dtype=jnp.int32)
    summary_pos = jnp.arange(summary_count, dtype=jnp.int32) * B + B - 1
    is_local = jnp.arange(2 * B + summary_count, dtype=jnp.int32) < 2 * B

    def one_block(local_index, query_part, key_prev, key_here, value_prev, value_here, grad_part):
        block_start = offset + local_index * B
        key_set = jnp.concatenate([key_prev, key_here, summary_key], axis=0)
        value_set = jnp.concatenate([value_prev, value_here, summary_value], axis=0)
        query_pos = block_start + steps_b
        key_pos = jnp.concatenate([block_start - B + steps_b, block_start + steps_b, summary_pos])
        near = (
            (key_pos[None, :] > query_pos[:, None] - B)
            & (key_pos[None, :] <= query_pos[:, None])
            & (key_pos[None, :] >= 0)
        )
        far_ok = key_pos[None, :] <= query_pos[:, None] - B
        allowed = jnp.where(is_local[None, :], near, far_ok)
        return attend_back(query_part, key_set, value_set, grad_part, allowed)

    grad_query, grad_keyset, grad_valset, log_total, inner_term = jax.vmap(one_block)(
        jnp.arange(block_count, dtype=jnp.int32),
        query_blocks,
        key_before,
        key_blocks,
        value_before,
        value_blocks,
        grad_blocks,
    )
    empty_grad = jnp.zeros((1, B, head_count, E), jnp.float32)
    own_key = grad_keyset[:, B : 2 * B] + jnp.concatenate([grad_keyset[1:, :B], empty_grad], axis=0)
    own_value = grad_valset[:, B : 2 * B] + jnp.concatenate(
        [grad_valset[1:, :B], empty_grad], axis=0
    )
    back_key, back_value = (
        passed_along(grad_keyset[0, :B].astype(jnp.bfloat16), "seq", -1).astype(jnp.float32),
        passed_along(grad_valset[0, :B].astype(jnp.bfloat16), "seq", -1).astype(jnp.float32),
    )
    own_key = own_key.at[block_count - 1].add(back_key)
    own_value = own_value.at[block_count - 1].add(back_value)
    summary_gk = jnp.sum(grad_keyset[:, 2 * B :], axis=0)
    summary_gv = jnp.sum(grad_valset[:, 2 * B :], axis=0)
    empty_sum = jnp.zeros_like(summary_gk)
    later_key, later_value = prefix(
        (summary_gk, summary_gv), "seq", add_pair, (empty_sum, empty_sum)
    )
    start_row = lax.axis_index("seq") * block_count
    mine_key = lax.dynamic_slice_in_dim(later_key + summary_gk, start_row, block_count, 0)
    mine_value = lax.dynamic_slice_in_dim(later_value + summary_gv, start_row, block_count, 0)
    own_key = own_key.at[:, B - 1].add(mine_key)
    own_value = own_value.at[:, B - 1].add(mine_value)
    return (
        grad_query.reshape(shard_len, feature_count).astype(jnp.bfloat16),
        own_key.reshape(shard_len, feature_count).astype(jnp.bfloat16),
        own_value.reshape(shard_len, feature_count).astype(jnp.bfloat16),
    )


def solution(mesh):
    return jax.shard_map(
        body,
        mesh=mesh,
        in_specs=(
            P(("dp", "seq"), "head"),
            P(("dp", "seq"), "head"),
            P(("dp", "seq"), "head"),
            P(("dp", "seq"), "head"),
        ),
        out_specs=(P(("dp", "seq"), "head"), P(("dp", "seq"), "head"), P(("dp", "seq"), "head")),
        check_vma=False,
    )
```

profile of v0, /device:TPU:0, one launch (start us, length us, event | category | flops | bytes accessed | tf_op | source)
XLA Modules:
  0.0 187.8 jit_solution(2531822382661108834)
XLA Ops:
  0.6 0.0 copy-start
  0.7 1.4 copy.41
  2.1 0.3 copy.42
  2.3 5.7 %collective-permute-start = (bf16[128,16,128]{2,0,1:T(8,128)(2,1)S(1)}, bf16[128,16,128]{2,0,1:T(8,128)(2,1)}, u32[]{:S(2)}, u32[]{:S(2)}) collective-permute-start(bf16[128,16,128]{2,0,1:T(8,128)(2,1)S(1)} %copy.42), channel_id=1, source_target_pairs={{0,4},{4,8},{8,12},{12,16},{16,20},{20,24},{24,28},{1,5},{5,9},{9,... | collective-permute-start | bytes 1572872 | tf_op jit(solution)/shard_map/ppermute | solution.py:14
  8.1 0.3 copy.48
  8.3 1.0 copy.49
  9.3 3.4 %collective-permute-start.1 = (bf16[128,16,128]{2,0,1:T(8,128)(2,1)}, bf16[128,16,128]{2,0,1:T(8,128)(2,1)}, u32[]{:S(2)}, u32[]{:S(2)}) collective-permute-start(bf16[128,16,128]{2,0,1:T(8,128)(2,1)} %copy.49), channel_id=1, source_target_pairs={{0,4},{4,8},{8,12},{12,16},{16,20},{20,24},{24,28},{1,5},{5,9},{9,... | collective-permute-start | bytes 1572872 | tf_op jit(solution)/shard_map/ppermute | solution.py:14
  12.8 0.2 slice.138
  13.0 1.0 copy.46
  14.0 0.2 slice.139
  14.2 1.0 copy.53
  15.2 0.2 copy.44
  15.4 40.1 %all-gather = bf16[8,1,16,128]{3,2,1,0:T(8,128)(2,1)S(1)} all-gather(bf16[1,1,16,128]{3,2,1,0:T(8,128)(2,1)S(1)} %copy.44), channel_id=2, replica_groups=mesh['seq'=8,'head'=2,'dp'=2] {'seq'}, dimensions={0}, use_global_device_ids=true | all-gather | bytes 36864 | tf_op jit(solution)/shard_map/all_gather | solution.py:97
  55.6 0.2 copy.51
  55.8 30.4 %all-gather.1 = bf16[8,1,16,128]{3,2,1,0:T(8,128)(2,1)S(1)} all-gather(bf16[1,1,16,128]{3,2,1,0:T(8,128)(2,1)S(1)} %copy.51), channel_id=3, replica_groups=mesh['seq'=8,'head'=2,'dp'=2] {'seq'}, dimensions={0}, use_global_device_ids=true | all-gather | bytes 36864 | tf_op jit(solution)/shard_map/all_gather | solution.py:98
  86.2 0.9 copy.75
  87.2 0.2 compare_select_fusion
  87.4 1.9 %fusion.24 = (f32[16,128]{1,0:T(8,128)S(1)}, f32[16,128,264]{1,2,0:T(8,128)S(1)}) fusion(bf16[1,8,16,128]{3,1,2,0:T(8,128)(2,1)S(1)} %bitcast.126, bf16[1,128,16,128]{3,1,2,0:T(8,128)(2,1)} %copy.46, bf16[1,128,16,128]{3,1,2,0:T(8,128)(2,1)} %bitcast.5, pred[128,264]{0,1:T(8,128)(4,1)S(1)} %compare_select_fusion, bf16[128,2048]{1,0:T(8,128)(2,1)S(1)} %copy-done), kind=kOutput, calls=%fused_computation.55 | convolution fusion | flops 143276032 | bytes 3810304 | tf_op jit(solution)/shard_map/vmap(qhe,khe->hqk)/dot_general | solution.py:36
  89.3 0.3 exponential_reduce_fusion
  89.7 0.7 copy-done.7
  90.4 2.9 %convolution_bitcast_fusion.1 = f32[16,128,128]{1,2,0:T(8,128)} fusion(bf16[1,8,16,128]{3,1,2,0:T(8,128)(2,1)S(1)} %bitcast.128, bf16[1,128,16,128]{3,1,2,0:T(8,128)(2,1)S(1)} %copy-done.7, bf16[1,128,16,128]{3,1,2,0:T(8,128)(2,1)} %bitcast.11, f32[16,128,264]{1,2,0:T(8,128)S(1)} %get-tuple-element.174, f32[16,128]{1,0:T(8,128)S(1)} %log_add_fusion), kind=kOutput, calls=%fused_computation.11 | convolution fusion | flops 142737408 | bytes 4300800 | tf_op jit(solution)/shard_map/vmap(hqk,khe->qhe)/dot_general | solution.py:65
  93.2 2.6 %copy.71 = f32[16,128,128]{2,0,1:T(8,128)} copy(f32[16,128,128]{1,2,0:T(8,128)} %convolution_bitcast_fusion.1) | data formatting | bytes 2097152
  95.8 1.7 multiply_reduce_fusion
  97.5 0.1 copy.72
  97.6 1.9 %fusion = bf16[16,128,264]{1,2,0:T(8,128)(2,1)S(1)} fusion(f32[16,128,264]{1,2,0:T(8,128)S(1)} %get-tuple-element.174, f32[16,128]{1,0:T(8,128)S(1)} %copy.72, f32[16,128]{1,0:T(8,128)S(1)} %log_add_fusion, bf16[1,8,16,128]{3,1,2,0:T(8,128)(2,1)S(1)} %bitcast.129, bf16[1,128,16,128]{3,1,2,0:T(8,128)(2,1)} %copy.53, bf16[1,128,16,128]{3,1,2,0:T(8,128)(2,1)} %bitcast.11, ...), kind=kOutput, calls=%fused_computation.3 | convolution fusion | flops 143818752 | bytes 4866048 | tf_op jit(solution)/shard_map/vmap(qhe,khe->hqk)/dot_general | solution.py:46
  99.6 0.7 multiply_bitcast_fusion
  100.3 1.0 fusion.3
  101.3 0.4 copy-done.2
  101.8 0.7 convolution_bitcast_fusion
  102.5 1.3 collective-permute-start.2
  103.9 35.6 %all_gather.16 = f32[8,8,16,128]{3,2,1,0:T(8,128)S(1)} all-gather(f32[1,8,16,128]{3,2,1,0:T(8,128)S(1)} %copy.56), channel_id=1, replica_groups=mesh['seq'=8,'head'=2,'dp'=2] {'seq'}, dimensions={0}, use_global_device_ids=true | all-gather | bytes 589824 | tf_op jit(solution)/shard_map/all_gather | solution.py:21
  139.5 31.6 %all_gather.17 = f32[8,8,16,128]{3,2,1,0:T(8,128)S(1)} all-gather(f32[1,8,16,128]{3,2,1,0:T(8,128)S(1)} %copy.58), channel_id=1, replica_groups=mesh['seq'=8,'head'=2,'dp'=2] {'seq'}, dimensions={0}, use_global_device_ids=true | all-gather | bytes 589824 | tf_op jit(solution)/shard_map/all_gather | solution.py:21
  171.1 0.4 while.18
  171.5 2.1 %fusion.4 = bf16[128,16,128]{2,0,1:T(8,128)(2,1)} fusion(f32[1,264,16,128]{3,1,2,0:T(8,128)} %copy-done.1), kind=kLoop, calls=%fused_computation.21 | loop fusion | bytes 1048576 | tf_op jit(solution)/shard_map/convert_element_type | solution.py:138
  173.7 1.3 collective-permute-start.3
  175.0 2.7 %fusion.2 = bf16[16,128,128]{2,1,0:T(8,128)(2,1)} fusion(bf16[16,128,264]{1,2,0:T(8,128)(2,1)S(1)} %copy-done.5, bf16[1,8,16,128]{3,1,2,0:T(8,128)(2,1)S(1)} %bitcast.127, bf16[1,128,16,128]{3,1,2,0:T(8,128)(2,1)} %copy.46, bf16[1,128,16,128]{3,1,2,0:T(8,128)(2,1)} %bitcast.5), kind=kOutput, calls=%fused_computation.12 | convolution fusion | flops 142180352 | bytes 2686976 | tf_op jit(solution)/shard_map/vmap(hqk,khe->qhe)/dot_general | solution.py:70
  177.6 2.0 %copy.63 = bf16[128,2048]{1,0:T(8,128)(2,1)} copy(bf16[128,2048]{0,1:T(8,128)(2,1)} %bitcast.125) | data formatting | bytes 1048576
  179.7 1.3 slice_add_fusion.1
  181.1 0.1 scatter-add.6
  181.2 0.1 convert_element_type.51
  181.3 0.3 copy.60
  181.6 1.0 copy.64
  182.6 2.4 %collective-permute-done.3 = bf16[128,16,128]{2,0,1:T(8,128)(2,1)S(1)} collective-permute-done((bf16[128,16,128]{2,0,1:T(8,128)(2,1)}, bf16[128,16,128]{2,0,1:T(8,128)(2,1)S(1)}, u32[]{:S(2)}, u32[]{:S(2)}) %collective-permute-start.3) | collective-permute-done | bytes 524320 | tf_op jit(solution)/shard_map/ppermute | solution.py:14
  184.9 1.3 slice_add_fusion
  186.3 0.1 scatter-add.9
  186.4 0.1 convert_element_type.54
  186.5 0.3 copy.62
  186.7 1.0 copy.65
  (42 shorter events, 0.5 us)
Async XLA Ops:
  0.6 86.7 %copy-start = (bf16[128,2048]{1,0:T(8,128)(2,1)S(1)}, bf16[128,2048]{1,0:T(8,128)(2,1)}, u32[]{:S(2)}) copy-start(bf16[128,2048]{1,0:T(8,128)(2,1)} %param.14) | copy-start | bytes 1572868
  0.6 7.4 %copy-start.6 = (bf16[128,2048]{1,0:T(8,128)(2,1)S(1)}, bf16[128,2048]{1,0:T(8,128)(2,1)}, u32[]{:S(2)}) copy-start(bf16[128,2048]{1,0:T(8,128)(2,1)} %param.16) | copy-start | bytes 1572868
  2.3 85.0 %collective-permute-start = (bf16[128,16,128]{2,0,1:T(8,128)(2,1)S(1)}, bf16[128,16,128]{2,0,1:T(8,128)(2,1)}, u32[]{:S(2)}, u32[]{:S(2)}) collective-permute-start(bf16[128,16,128]{2,0,1:T(8,128)(2,1)S(1)} %copy.42), channel_id=1, source_target_pairs={{0,4},{4,8},{8,12},{12,16},{16,20},{20,24},{24,28},{1,5},{5,9},{9,... | collective-permute-start | bytes 1572872 | tf_op jit(solution)/shard_map/ppermute | solution.py:14
  9.3 80.3 %collective-permute-start.1 = (bf16[128,16,128]{2,0,1:T(8,128)(2,1)}, bf16[128,16,128]{2,0,1:T(8,128)(2,1)}, u32[]{:S(2)}, u32[]{:S(2)}) collective-permute-start(bf16[128,16,128]{2,0,1:T(8,128)(2,1)} %copy.49), channel_id=1, source_target_pairs={{0,4},{4,8},{8,12},{12,16},{16,20},{20,24},{24,28},{1,5},{5,9},{9,... | collective-permute-start | bytes 1572872 | tf_op jit(solution)/shard_map/ppermute | solution.py:14
  13.0 73.3 %copy-start.3 = (bf16[128,2048]{1,0:T(8,128)(2,1)S(1)}, bf16[128,2048]{1,0:T(8,128)(2,1)}, u32[]{:S(2)}) copy-start(bf16[128,2048]{1,0:T(8,128)(2,1)} %param.17) | copy-start | bytes 1572868
  89.3 1.0 copy-start.7
  99.5 1.8 copy-start.4
  100.3 1.5 copy-start.2
  102.5 37.0 %copy-start.1 = (f32[1,264,16,128]{3,1,2,0:T(8,128)}, f32[1,264,16,128]{3,1,2,0:T(8,128)S(1)}, u32[]{:S(2)}) copy-start(f32[1,264,16,128]{3,1,2,0:T(8,128)S(1)} %convolution_bitcast_fusion) | copy-start | bytes 6488068
  102.5 77.2 %collective-permute-start.2 = (bf16[128,16,128]{2,0,1:T(8,128)(2,1)}, bf16[128,16,128]{2,0,1:T(8,128)(2,1)S(1)}, u32[]{:S(2)}, u32[]{:S(2)}) collective-permute-start(bf16[128,16,128]{2,0,1:T(8,128)(2,1)} %fusion.3), channel_id=1, source_target_pairs={{4,0},{8,4},{12,8},{16,12},{20,16},{24,20},{28,24},{5,1},{9,5},{13... | collective-permute-start | bytes 1572872 | tf_op jit(solution)/shard_map/ppermute | solution.py:14
  139.5 35.5 %copy-start.5 = (bf16[16,128,264]{1,2,0:T(8,128)(2,1)S(1)}, bf16[16,128,264]{1,2,0:T(8,128)(2,1)}, u32[]{:S(2)}) copy-start(bf16[16,128,264]{1,2,0:T(8,128)(2,1)} %copy-done.4) | copy-start | bytes 3244036
  173.7 11.3 %collective-permute-start.3 = (bf16[128,16,128]{2,0,1:T(8,128)(2,1)}, bf16[128,16,128]{2,0,1:T(8,128)(2,1)S(1)}, u32[]{:S(2)}, u32[]{:S(2)}) collective-permute-start(bf16[128,16,128]{2,0,1:T(8,128)(2,1)} %fusion.4), channel_id=1, source_target_pairs={{4,0},{8,4},{12,8},{16,12},{20,16},{24,20},{28,24},{5,1},{9,5},{13... | collective-permute-start | bytes 1572872 | tf_op jit(solution)/shard_map/ppermute | solution.py:14
where the time goes:
time: 188 us
  blocking collectives  138 us (73%)
  local copies, waits for them, and re-layouts  18.6 us (10%)
  starting transfers between devices  11.7 us (6%)
  matrix products  10.8 us (6%)
  other arithmetic  5.32 us (3%)
  waiting for transfers between devices  2.37 us (1%)
    all_gather x2, blocking collectives, prefix(): gathered = jax.tree.map(lambda a: lax.all_gather(a, axis), part)  67.2 us
    all_gather x1, blocking collectives, body(): lax.all_gather(strided_key, 'seq', axis=0, tiled=True)  40.1 us
    all_gather x1, blocking collectives, body(): lax.all_gather(strided_value, 'seq', axis=0, tiled=True)  30.4 us
    ppermute x4, starting transfers between devices, passed_along(): return lax.ppermute(block, axis, route)  11.7 us
    unnamed x23, local copies, waits for them, and re-layouts  10.4 us
  transfers between devices with their start and end apart: 4, of which 1 were waited for; matrix products, arithmetic and copies ran while one was open for 9% of the time, Pallas kernels for 0%

commit v1 on v0

--- a/solution.py
+++ b/solution.py
@@ -6,6 +6,24 @@
 E = 128
 B = 128
 masked_value = -1e30
+
+
+def ring_gather(shard, axis, dim):
+    ways, here, step = (lax.axis_size(axis), lax.axis_index(axis), shard.shape[dim])
+    shape = [n * ways if d == dim else n for d, n in enumerate(shard.shape)]
+    full = lax.dynamic_update_slice_in_dim(
+        jnp.zeros(shape, shard.dtype), shard, here * step, axis=dim
+    )
+    going_up = going_down = shard
+    for far in range(1, ways // 2 + 1):
+        going_up = lax.ppermute(going_up, axis, [(d, (d + 1) % ways) for d in range(ways)])
+        full = lax.dynamic_update_slice_in_dim(full, going_up, (here - far) % ways * step, axis=dim)
+        if 2 * far < ways:
+            going_down = lax.ppermute(going_down, axis, [(d, (d - 1) % ways) for d in range(ways)])
+            full = lax.dynamic_update_slice_in_dim(
+                full, going_down, (here + far) % ways * step, axis=dim
+            )
+    return full
 
 
 def passed_along(block, axis, distance):
@@ -95,7 +113,7 @@
     strided_value = value_blocks[:, B - 1]
     summary_key, summary_value = (
         lax.all_gather(strided_key, "seq", axis=0, tiled=True),
-        lax.all_gather(strided_value, "seq", axis=0, tiled=True),
+        ring_gather(strided_value, "seq", 0),
     )
     summary_count = summary_key.shape[0]
     key_before = jnp.concatenate([halo_key[None], key_blocks[:-1]], axis=0)

time: 188 us -> 182 us (0.968)
  blocking collectives: 138 us -> 102 us
  waiting for transfers between devices: 2.37 us -> 18.5 us
  starting transfers between devices: 11.7 us -> 24.6 us
    all_gather x1 -> x0, blocking collectives: 30.4 us -> none  [body(): lax.all_gather(strided_value, 'seq', axis=0, tiled=True)]
    ppermute x0 -> x7, waiting for transfers between devices: none -> 16.3 us  [the longest x4 16.3 us: ring_gather(): lax.ppermute(going_up, axis, [(d, (d + 1) % ways) for d in range(ways)])]
    ppermute x0 -> x7, starting transfers between devices: none -> 15.9 us  [the longest x3 10.4 us: ring_gather(): lax.ppermute(going_down, axis, [(d, (d - 1) % ways) for d in range(ways)])]
    all_gather x1, blocking collectives: 40.1 us -> 30.4 us  [body(): lax.all_gather(strided_key, 'seq', axis=0, tiled=True)]
    all_gather x2, blocking collectives: 67.2 us -> 71.3 us  [prefix(): gathered = jax.tree.map(lambda a: lax.all_gather(a, axis), part)]
    ppermute x4, starting transfers between devices: 11.7 us -> 8.67 us  [passed_along(): return lax.ppermute(block, axis, route)]
    unnamed x23 -> x28, local copies, waits for them, and re-layouts: 10.4 us -> 11.3 us
  transfers between devices with their start and end apart: 4 -> 11, of which waited for: 1 -> 3; matrix products, arithmetic and copies ran while one was open for 9% -> 9% of each run, Pallas kernels for 0% -> 0%
where the time goes in v1:
time: 182 us; the launch traced here: 181 us
  blocking collectives  102 us (56%)
  starting transfers between devices  24.6 us (14%)
  local copies, waits for them, and re-layouts  18.7 us (10%)
  waiting for transfers between devices  18.5 us (10%)
  matrix products  10.8 us (6%)
  other arithmetic  5.47 us (3%)
    all_gather x2, blocking collectives, prefix(): gathered = jax.tree.map(lambda a: lax.all_gather(a, axis), part)  71.3 us
    all_gather x1, blocking collectives, body(): lax.all_gather(strided_key, 'seq', axis=0, tiled=True)  30.4 us
    ppermute x4, waiting for transfers between devices, ring_gather(): lax.ppermute(going_up, axis, [(d, (d + 1) % ways) for d in range(ways)])  16.3 us
    unnamed x28, local copies, waits for them, and re-layouts  11.3 us
    ppermute x3, starting transfers between devices, ring_gather(): lax.ppermute(going_down, axis, [(d, (d - 1) % ways) for d in range(ways)])  10.4 us
    ppermute x4, starting transfers between devices, passed_along(): return lax.ppermute(block, axis, route)  8.67 us
    ppermute x4, starting transfers between devices, ring_gather(): lax.ppermute(going_up, axis, [(d, (d + 1) % ways) for d in range(ways)])  5.56 us
  transfers between devices with their start and end apart: 11, of which 3 were waited for; matrix products, arithmetic and copies ran while one was open for 9% of the time, Pallas kernels for 0%

profile of v1, /device:TPU:0, one launch (start us, length us, event | category | flops | bytes accessed | tf_op | source)
XLA Modules:
  0.0 181.2 jit_solution(17582025751792916397)
XLA Ops:
  0.7 1.4 copy.257
  2.1 0.3 copy.268
  2.4 3.0 %collective-permute-start.2 = (bf16[1,16,128]{2,1,0:T(8,128)(2,1)S(1)}, bf16[1,16,128]{2,1,0:T(8,128)(2,1)S(1)}, u32[]{:S(2)}, u32[]{:S(2)}) collective-permute-start(bf16[1,16,128]{2,1,0:T(8,128)(2,1)S(1)} %bitcast.141), channel_id=1, source_target_pairs={{0,4},{4,8},{8,12},{12,16},{16,20},{20,24},{24,28},{28,0},{1,5},{5... | collective-permute-start | bytes 12296 | tf_op jit(solution)/shard_map/ppermute | solution.py:19
  5.4 3.1 %collective-permute-start.3 = (bf16[1,16,128]{2,1,0:T(8,128)(2,1)S(1)}, bf16[1,16,128]{2,1,0:T(8,128)(2,1)S(1)}, u32[]{:S(2)}, u32[]{:S(2)}) collective-permute-start(bf16[1,16,128]{2,1,0:T(8,128)(2,1)S(1)} %bitcast.142), channel_id=1, source_target_pairs={{0,28},{4,0},{8,4},{12,8},{16,12},{20,16},{24,20},{28,24},{1,29},{... | collective-permute-start | bytes 12296 | tf_op jit(solution)/shard_map/ppermute | solution.py:22
  8.5 0.3 copy.250
  8.8 0.3 copy.251
  9.1 1.5 collective-permute-start
  10.6 1.0 copy.258
  11.6 4.6 %collective-permute-start.1 = (bf16[128,16,128]{2,0,1:T(8,128)(2,1)}, bf16[128,16,128]{2,0,1:T(8,128)(2,1)}, u32[]{:S(2)}, u32[]{:S(2)}) collective-permute-start(bf16[128,16,128]{2,0,1:T(8,128)(2,1)} %copy.258), channel_id=1, source_target_pairs={{0,4},{4,8},{8,12},{12,16},{16,20},{20,24},{24,28},{1,5},{5,9},{9,... | collective-permute-start | bytes 1572872 | tf_op jit(solution)/shard_map/ppermute | solution.py:32
  16.4 0.2 compare_select_fusion
  16.5 0.2 slice.138
  16.8 0.2 copy.253
  17.0 4.8 %collective-permute-start.5 = (bf16[1,16,128]{2,1,0:T(8,128)(2,1)S(1)}, bf16[1,16,128]{2,1,0:T(8,128)(2,1)S(1)}, u32[]{:S(2)}, u32[]{:S(2)}) collective-permute-start(bf16[1,16,128]{2,1,0:T(8,128)(2,1)S(1)} %collective-permute-done.3), channel_id=1, source_target_pairs={{0,28},{4,0},{8,4},{12,8},{16,12},{20,16},{24,20},{28,24},{1,29},{... | collective-permute-start | bytes 12296 | tf_op jit(solution)/shard_map/ppermute | solution.py:22
  21.7 11.4 %collective-permute-done.4 = bf16[1,16,128]{2,1,0:T(8,128)(2,1)S(1)} collective-permute-done((bf16[1,16,128]{2,1,0:T(8,128)(2,1)S(1)}, bf16[1,16,128]{2,1,0:T(8,128)(2,1)S(1)}, u32[]{:S(2)}, u32[]{:S(2)}) %collective-permute-start.4) | collective-permute-done | bytes 4128 | tf_op jit(solution)/shard_map/ppermute | solution.py:19
  33.2 2.5 %collective-permute-start.6 = (bf16[1,16,128]{2,1,0:T(8,128)(2,1)S(1)}, bf16[1,16,128]{2,1,0:T(8,128)(2,1)S(1)}, u32[]{:S(2)}, u32[]{:S(2)}) collective-permute-start(bf16[1,16,128]{2,1,0:T(8,128)(2,1)S(1)} %collective-permute-done.4), channel_id=1, source_target_pairs={{0,4},{4,8},{8,12},{12,16},{16,20},{20,24},{24,28},{28,0},{1,5},{5... | collective-permute-start | bytes 12296 | tf_op jit(solution)/shard_map/ppermute | solution.py:19
  35.6 30.4 %all-gather = bf16[8,1,16,128]{3,2,1,0:T(8,128)(2,1)S(1)} all-gather(bf16[1,1,16,128]{3,2,1,0:T(8,128)(2,1)S(1)} %copy.253), channel_id=2, replica_groups=mesh['seq'=8,'head'=2,'dp'=2] {'seq'}, dimensions={0}, use_global_device_ids=true | all-gather | bytes 36864 | tf_op jit(solution)/shard_map/all_gather | solution.py:115
  66.0 1.0 copy.255
  67.1 2.5 %collective-permute-start.7 = (bf16[1,16,128]{2,1,0:T(8,128)(2,1)S(1)}, bf16[1,16,128]{2,1,0:T(8,128)(2,1)S(1)}, u32[]{:S(2)}, u32[]{:S(2)}) collective-permute-start(bf16[1,16,128]{2,1,0:T(8,128)(2,1)S(1)} %collective-permute-done.5), channel_id=1, source_target_pairs={{0,28},{4,0},{8,4},{12,8},{16,12},{20,16},{24,20},{28,24},{1,29},{... | collective-permute-start | bytes 12296 | tf_op jit(solution)/shard_map/ppermute | solution.py:22
  69.6 0.9 copy.291
  71.0 4.9 %collective-permute-done.8 = bf16[1,16,128]{2,1,0:T(8,128)(2,1)S(1)} collective-permute-done((bf16[1,16,128]{2,1,0:T(8,128)(2,1)S(1)}, bf16[1,16,128]{2,1,0:T(8,128)(2,1)S(1)}, u32[]{:S(2)}, u32[]{:S(2)}) %collective-permute-start.8) | collective-permute-done | bytes 4128 | tf_op jit(solution)/shard_map/ppermute | solution.py:19
  76.0 0.8 copy-done.9
  76.8 1.9 %fusion.24 = (f32[16,128]{1,0:T(8,128)S(1)}, f32[16,128,264]{1,2,0:T(8,128)S(1)}) fusion(bf16[1,8,16,128]{3,1,2,0:T(8,128)(2,1)S(1)} %bitcast.132, bf16[1,128,16,128]{3,1,2,0:T(8,128)(2,1)} %copy.255, bf16[1,128,16,128]{3,1,2,0:T(8,128)(2,1)} %bitcast.143, pred[128,264]{0,1:T(8,128)(4,1)S(1)} %compare_select_fusion, bf16[128,2048]{1,0:T(8,128)(2,1)S(1)} %copy-done), kind=kOutput, calls=%fused_computation.55 | convolution fusion | flops 143276032 | bytes 3810304 | tf_op jit(solution)/shard_map/vmap(qhe,khe->hqk)/dot_general | solution.py:54
  78.7 0.3 exponential_reduce_fusion
  79.0 0.7 copy-done.7
  79.7 2.8 %convolution_bitcast_fusion.1 = f32[16,128,128]{1,2,0:T(8,128)} fusion(bf16[1,8,16,128]{3,1,2,0:T(8,128)(2,1)S(1)} %dynamic_update_slice.39, bf16[1,128,16,128]{3,1,2,0:T(8,128)(2,1)S(1)} %copy-done.7, bf16[1,128,16,128]{3,1,2,0:T(8,128)(2,1)} %bitcast.11, f32[16,128,264]{1,2,0:T(8,128)S(1)} %get-tuple-element.237, f32[16,128]{1,0:T(8,128)S(1)} %log_add_fusion), kind=kOutput, calls=%fused_computation.11 | convolution fusion | flops 142737408 | bytes 4300800 | tf_op jit(solution)/shard_map/vmap(hqk,khe->qhe)/dot_general | solution.py:83
  82.5 2.6 %copy.286 = f32[16,128,128]{2,0,1:T(8,128)} copy(f32[16,128,128]{1,2,0:T(8,128)} %convolution_bitcast_fusion.1) | data formatting | bytes 2097152
  85.2 1.7 multiply_reduce_fusion
  86.9 1.9 %fusion = bf16[16,128,264]{1,2,0:T(8,128)(2,1)S(1)} fusion(f32[16,128,264]{1,2,0:T(8,128)S(1)} %get-tuple-element.237, f32[16,128]{1,0:T(8,128)S(1)} %copy.287, f32[16,128]{1,0:T(8,128)S(1)} %log_add_fusion, bf16[1,8,16,128]{3,1,2,0:T(8,128)(2,1)S(1)} %dynamic_update_slice.39, bf16[1,128,16,128]{3,1,2,0:T(8,128)(2,1)} %copy-done.6, ...), kind=kOutput, calls=%fused_computation.3 | convolution fusion | flops 143818752 | bytes 4866048 | tf_op jit(solution)/shard_map/vmap(qhe,khe->hqk)/dot_general | solution.py:64
  88.9 0.7 multiply_bitcast_fusion
  89.6 1.0 fusion.3
  90.7 0.5 copy-done.2
  91.2 0.7 convolution_bitcast_fusion
  91.9 1.3 collective-permute-start.9
  93.2 36.9 %all_gather.12 = f32[8,8,16,128]{3,2,1,0:T(8,128)S(1)} all-gather(f32[1,8,16,128]{3,2,1,0:T(8,128)S(1)} %copy.271), channel_id=1, replica_groups=mesh['seq'=8,'head'=2,'dp'=2] {'seq'}, dimensions={0}, use_global_device_ids=true | all-gather | bytes 589824 | tf_op jit(solution)/shard_map/all_gather | solution.py:39
  130.1 34.4 %all_gather.13 = f32[8,8,16,128]{3,2,1,0:T(8,128)S(1)} all-gather(f32[1,8,16,128]{3,2,1,0:T(8,128)S(1)} %copy.273), channel_id=1, replica_groups=mesh['seq'=8,'head'=2,'dp'=2] {'seq'}, dimensions={0}, use_global_device_ids=true | all-gather | bytes 589824 | tf_op jit(solution)/shard_map/all_gather | solution.py:39
  164.6 0.4 while.18
  165.0 2.1 %fusion.4 = bf16[128,16,128]{2,0,1:T(8,128)(2,1)} fusion(f32[1,264,16,128]{3,1,2,0:T(8,128)} %copy-done.1), kind=kLoop, calls=%fused_computation.21 | loop fusion | bytes 1048576 | tf_op jit(solution)/shard_map/convert_element_type | solution.py:156
  167.1 1.3 collective-permute-start.10
  168.4 2.7 %fusion.2 = bf16[16,128,128]{2,1,0:T(8,128)(2,1)} fusion(bf16[16,128,264]{1,2,0:T(8,128)(2,1)S(1)} %copy-done.5, bf16[1,8,16,128]{3,1,2,0:T(8,128)(2,1)S(1)} %bitcast.133, bf16[1,128,16,128]{3,1,2,0:T(8,128)(2,1)} %copy.255, bf16[1,128,16,128]{3,1,2,0:T(8,128)(2,1)} %bitcast.144), kind=kOutput, calls=%fused_computation.12 | convolution fusion | flops 142180352 | bytes 2686976 | tf_op jit(solution)/shard_map/vmap(hqk,khe->qhe)/dot_general | solution.py:88
  171.1 2.0 %copy.278 = bf16[128,2048]{1,0:T(8,128)(2,1)} copy(bf16[128,2048]{0,1:T(8,128)(2,1)} %bitcast.131) | data formatting | bytes 1048576
  173.2 1.5 slice_add_fusion.1
  174.9 0.3 copy.275
  175.2 1.0 copy.279
  176.2 2.2 %collective-permute-done.10 = bf16[128,16,128]{2,0,1:T(8,128)(2,1)S(1)} collective-permute-done((bf16[128,16,128]{2,0,1:T(8,128)(2,1)}, bf16[128,16,128]{2,0,1:T(8,128)(2,1)S(1)}, u32[]{:S(2)}, u32[]{:S(2)}) %collective-permute-start.10) | collective-permute-done | bytes 524320 | tf_op jit(solution)/shard_map/ppermute | solution.py:32
  178.4 1.3 slice_add_fusion
  179.8 0.1 convert_element_type.54
  179.9 0.3 copy.277
  180.2 1.0 copy.280
  (74 shorter events, 1.3 us)
Async XLA Ops:
  0.6 76.1 %copy-start = (bf16[128,2048]{1,0:T(8,128)(2,1)S(1)}, bf16[128,2048]{1,0:T(8,128)(2,1)}, u32[]{:S(2)}) copy-start(bf16[128,2048]{1,0:T(8,128)(2,1)} %param.14) | copy-start | bytes 1572868
  0.6 7.9 %copy-start.8 = (bf16[128,2048]{1,0:T(8,128)(2,1)S(1)}, bf16[128,2048]{1,0:T(8,128)(2,1)}, u32[]{:S(2)}) copy-start(bf16[128,2048]{1,0:T(8,128)(2,1)} %param.15) | copy-start | bytes 1572868
  2.3 6.4 %copy-start.6 = (bf16[1,128,16,128]{3,1,2,0:T(8,128)(2,1)}, bf16[1,128,16,128]{3,1,2,0:T(8,128)(2,1)S(1)}, u32[]{:S(2)}) copy-start(bf16[1,128,16,128]{3,1,2,0:T(8,128)(2,1)S(1)} %copy.268) | copy-start | bytes 1572868
  2.4 13.9 %collective-permute-start.2 = (bf16[1,16,128]{2,1,0:T(8,128)(2,1)S(1)}, bf16[1,16,128]{2,1,0:T(8,128)(2,1)S(1)}, u32[]{:S(2)}, u32[]{:S(2)}) collective-permute-start(bf16[1,16,128]{2,1,0:T(8,128)(2,1)S(1)} %bitcast.141), channel_id=1, source_target_pairs={{0,4},{4,8},{8,12},{12,16},{16,20},{20,24},{24,28},{28,0},{1,5},{5... | collective-permute-start | bytes 12296 | tf_op jit(solution)/shard_map/ppermute | solution.py:19
  5.4 11.6 %collective-permute-start.3 = (bf16[1,16,128]{2,1,0:T(8,128)(2,1)S(1)}, bf16[1,16,128]{2,1,0:T(8,128)(2,1)S(1)}, u32[]{:S(2)}, u32[]{:S(2)}) collective-permute-start(bf16[1,16,128]{2,1,0:T(8,128)(2,1)S(1)} %bitcast.142), channel_id=1, source_target_pairs={{0,28},{4,0},{8,4},{12,8},{16,12},{20,16},{24,20},{28,24},{1,29},{... | collective-permute-start | bytes 12296 | tf_op jit(solution)/shard_map/ppermute | solution.py:22
  9.1 60.5 %copy-start.3 = (bf16[128,2048]{1,0:T(8,128)(2,1)S(1)}, bf16[128,2048]{1,0:T(8,128)(2,1)}, u32[]{:S(2)}) copy-start(bf16[128,2048]{1,0:T(8,128)(2,1)} %param.17) | copy-start | bytes 1572868
  9.1 66.8 %collective-permute-start = (bf16[128,16,128]{2,0,1:T(8,128)(2,1)S(1)}, bf16[128,16,128]{2,0,1:T(8,128)(2,1)S(1)}, u32[]{:S(2)}, u32[]{:S(2)}) collective-permute-start(bf16[128,16,128]{2,0,1:T(8,128)(2,1)S(1)} %copy.251), channel_id=1, source_target_pairs={{0,4},{4,8},{8,12},{12,16},{16,20},{20,24},{24,28},{1,5},{5,9},{9,... | collective-permute-start | bytes 1572872 | tf_op jit(solution)/shard_map/ppermute | solution.py:32
  11.6 67.5 %collective-permute-start.1 = (bf16[128,16,128]{2,0,1:T(8,128)(2,1)}, bf16[128,16,128]{2,0,1:T(8,128)(2,1)}, u32[]{:S(2)}, u32[]{:S(2)}) collective-permute-start(bf16[128,16,128]{2,0,1:T(8,128)(2,1)} %copy.258), channel_id=1, source_target_pairs={{0,4},{4,8},{8,12},{12,16},{16,20},{20,24},{24,28},{1,5},{5,9},{9,... | collective-permute-start | bytes 1572872 | tf_op jit(solution)/shard_map/ppermute | solution.py:32
  16.3 16.9 %collective-permute-start.4 = (bf16[1,16,128]{2,1,0:T(8,128)(2,1)S(1)}, bf16[1,16,128]{2,1,0:T(8,128)(2,1)S(1)}, u32[]{:S(2)}, u32[]{:S(2)}) collective-permute-start(bf16[1,16,128]{2,1,0:T(8,128)(2,1)S(1)} %collective-permute-done.2), channel_id=1, source_target_pairs={{0,4},{4,8},{8,12},{12,16},{16,20},{20,24},{24,28},{28,0},{1,5},{5... | collective-permute-start | bytes 12296 | tf_op jit(solution)/shard_map/ppermute | solution.py:19
  17.0 50.1 %collective-permute-start.5 = (bf16[1,16,128]{2,1,0:T(8,128)(2,1)S(1)}, bf16[1,16,128]{2,1,0:T(8,128)(2,1)S(1)}, u32[]{:S(2)}, u32[]{:S(2)}) collective-permute-start(bf16[1,16,128]{2,1,0:T(8,128)(2,1)S(1)} %collective-permute-done.3), channel_id=1, source_target_pairs={{0,28},{4,0},{8,4},{12,8},{16,12},{20,16},{24,20},{28,24},{1,29},{... | collective-permute-start | bytes 12296 | tf_op jit(solution)/shard_map/ppermute | solution.py:22
  33.2 36.4 %collective-permute-start.6 = (bf16[1,16,128]{2,1,0:T(8,128)(2,1)S(1)}, bf16[1,16,128]{2,1,0:T(8,128)(2,1)S(1)}, u32[]{:S(2)}, u32[]{:S(2)}) collective-permute-start(bf16[1,16,128]{2,1,0:T(8,128)(2,1)S(1)} %collective-permute-done.4), channel_id=1, source_target_pairs={{0,4},{4,8},{8,12},{12,16},{16,20},{20,24},{24,28},{28,0},{1,5},{5... | collective-permute-start | bytes 12296 | tf_op jit(solution)/shard_map/ppermute | solution.py:19
  67.1 3.8 %collective-permute-start.7 = (bf16[1,16,128]{2,1,0:T(8,128)(2,1)S(1)}, bf16[1,16,128]{2,1,0:T(8,128)(2,1)S(1)}, u32[]{:S(2)}, u32[]{:S(2)}) collective-permute-start(bf16[1,16,128]{2,1,0:T(8,128)(2,1)S(1)} %collective-permute-done.5), channel_id=1, source_target_pairs={{0,28},{4,0},{8,4},{12,8},{16,12},{20,16},{24,20},{28,24},{1,29},{... | collective-permute-start | bytes 12296 | tf_op jit(solution)/shard_map/ppermute | solution.py:22
  69.6 6.3 %collective-permute-start.8 = (bf16[1,16,128]{2,1,0:T(8,128)(2,1)S(1)}, bf16[1,16,128]{2,1,0:T(8,128)(2,1)S(1)}, u32[]{:S(2)}, u32[]{:S(2)}) collective-permute-start(bf16[1,16,128]{2,1,0:T(8,128)(2,1)S(1)} %collective-permute-done.6), channel_id=1, source_target_pairs={{0,4},{4,8},{8,12},{12,16},{16,20},{20,24},{24,28},{28,0},{1,5},{5... | collective-permute-start | bytes 12296 | tf_op jit(solution)/shard_map/ppermute | solution.py:19
  76.0 0.8 copy-start.9
  78.7 1.0 copy-start.7
  88.9 1.8 copy-start.4
  89.6 1.5 copy-start.2
  91.9 38.2 %copy-start.1 = (f32[1,264,16,128]{3,1,2,0:T(8,128)}, f32[1,264,16,128]{3,1,2,0:T(8,128)S(1)}, u32[]{:S(2)}) copy-start(f32[1,264,16,128]{3,1,2,0:T(8,128)S(1)} %convolution_bitcast_fusion) | copy-start | bytes 6488068
  91.9 81.3 %collective-permute-start.9 = (bf16[128,16,128]{2,0,1:T(8,128)(2,1)}, bf16[128,16,128]{2,0,1:T(8,128)(2,1)}, u32[]{:S(2)}, u32[]{:S(2)}) collective-permute-start(bf16[128,16,128]{2,0,1:T(8,128)(2,1)} %fusion.3), channel_id=1, source_target_pairs={{4,0},{8,4},{12,8},{16,12},{20,16},{24,20},{28,24},{5,1},{9,5},{13... | collective-permute-start | bytes 1572872 | tf_op jit(solution)/shard_map/ppermute | solution.py:32
  130.1 38.3 %copy-start.5 = (bf16[16,128,264]{1,2,0:T(8,128)(2,1)S(1)}, bf16[16,128,264]{1,2,0:T(8,128)(2,1)}, u32[]{:S(2)}) copy-start(bf16[16,128,264]{1,2,0:T(8,128)(2,1)} %copy-done.4) | copy-start | bytes 3244036
  167.1 11.3 %collective-permute-start.10 = (bf16[128,16,128]{2,0,1:T(8,128)(2,1)}, bf16[128,16,128]{2,0,1:T(8,128)(2,1)S(1)}, u32[]{:S(2)}, u32[]{:S(2)}) collective-permute-start(bf16[128,16,128]{2,0,1:T(8,128)(2,1)} %fusion.4), channel_id=1, source_target_pairs={{4,0},{8,4},{12,8},{16,12},{20,16},{24,20},{28,24},{5,1},{9,5},{13... | collective-permute-start | bytes 1572872 | tf_op jit(solution)/shard_map/ppermute | solution.py:32
